TPU v7x, 256 devices: a whole 4x4x8 slice. The times are simulated.
256 devices in a mesh: var: 32 (over x, z), dp: 2 (over core), segment: 4 (over y).
Axes of the slice: x: 4, y: 4, z: 8, core: 2. Of those that a mesh axis runs over, the one named last changes fastest.
Arguments:
- queries: bfloat16 [2, 4, 32, 256, 1024], P('dp', 'segment', 'var'), parts along dimension 0, may hold values from -22 to 22
- keys: bfloat16 [2, 4, 32, 256, 1024], P('dp', 'segment', 'var'), parts along dimension 0, may hold values from -22 to 22
- values: bfloat16 [2, 4, 32, 256, 1024], P('dp', 'segment', 'var'), parts along dimension 0, may hold values from -6 to 6
- out_grad: bfloat16 [2, 4, 32, 256, 1024], P('dp', 'segment', 'var'), parts along dimension 0, may hold values from -96 to 96
- proj_weight: bfloat16 [4, 2048, 3072], P('segment', 'var'), may hold values from -0.125 to 0.125
- links: int32 [32, 9], replicated, may hold values from -1 to 31, as said below
Outputs:
- passed: bfloat16 [2, 4, 32, 256, 2048], P('dp', 'segment', 'var'), parts along dimension 0
There are 2 independent parts, one for each index of `dp`. A program takes and returns all parts, laid end to end along the dimension named above; an argument that names none is the same for every part. Nothing has to cross between parts.
Inputs may be any that keep to these rules, and one draw needn't show every extreme that they name: `links`: row v lists v itself and some of the 8 variables at cyclic distance 1 to 4 from v (indices modulo 32), each at most once, listed first in order of signed offset, the remaining entries -1; some variable lists all 9.
All inputs are finite; a program needn't handle non-finite values.
Results may differ from a plain program's by a relative error of at most 0.007.
Values may be sent and summed in bfloat16 or wider, within the bound.
A program may use at most 256 MiB of HBM per device.

v0:
```python
import math

import jax
import jax.numpy as jnp
from jax import lax
from jax.sharding import PartitionSpec as P

HEADS = 16
CAUSAL_BLOCK = 128


neg_big = -1e30


def passed_along(block, axis, distance):
    devices = range(lax.axis_size(axis))
    route = [((i - distance) % len(devices), i) for i in devices]
    return lax.ppermute(block, axis, route)


def block_terms(own_query, own_grad, key_block, value_block, allowed, score_scale):
    scores = (
        jnp.einsum("phe,qhe->hpq", own_query, key_block, preferred_element_type=jnp.float32)
        * score_scale
    )
    scores = jnp.where(allowed[None], scores, neg_big)
    grad_attn = jnp.einsum(
        "phe,qhe->hpq", own_grad, value_block, preferred_element_type=jnp.float32
    )
    return (scores, grad_attn)


def shards(queries, keys, values, out_grad, proj_weight, links):
    patches = queries.shape[3]
    feature_width = queries.shape[4]
    head_size = feature_width // HEADS
    score_scale = 1.0 / math.sqrt(head_size)
    token_shape = (patches, HEADS, head_size)
    own_query = queries.reshape(token_shape)
    own_grad = out_grad.reshape(token_shape)
    own_pair = jnp.stack(
        [keys.reshape(patches, feature_width), values.reshape(patches, feature_width)]
    )
    var_count = lax.axis_size("var")
    reach = min(4, (var_count - 1) // 2)
    own_index = lax.axis_index("var")
    own_links = lax.dynamic_index_in_dim(links, own_index, 0, keepdims=False)
    block_index = jnp.arange(patches, dtype=jnp.int32) // CAUSAL_BLOCK
    causal = block_index[:, None] >= block_index[None, :]
    fetched = [(0, own_pair)]
    for distance in range(1, reach + 1):
        from_below = passed_along(own_pair, "var", distance)
        from_above = passed_along(own_pair, "var", -distance)
        fetched.append((-distance, from_below))
        fetched.append((distance, from_above))
    blocks = []
    for offset, pair_block in fetched:
        linked = jnp.any(own_links == (own_index + offset) % var_count)
        blocks.append(
            (
                offset,
                pair_block[0].reshape(token_shape),
                pair_block[1].reshape(token_shape),
                causal & linked,
            )
        )
    row_max = jnp.full((HEADS, patches), neg_big, jnp.float32)
    row_sum = jnp.zeros((HEADS, patches), jnp.float32)
    weighted = jnp.zeros((HEADS, patches), jnp.float32)
    for offset, key_block, value_block, allowed in blocks:
        scores, grad_attn = block_terms(
            own_query, own_grad, key_block, value_block, allowed, score_scale
        )
        new_max = jnp.maximum(row_max, scores.max(axis=2))
        shrink = jnp.exp(row_max - new_max)
        attention = jnp.exp(scores - new_max[:, :, None])
        row_sum = row_sum * shrink + attention.sum(axis=2)
        weighted = weighted * shrink + (attention * grad_attn).sum(axis=2)
        row_max = new_max
    log_total = row_max + jnp.log(row_sum)
    row_delta = weighted / row_sum
    grad_query = jnp.zeros(token_shape, jnp.float32)
    summed = jnp.zeros((2, patches, feature_width), jnp.float32)
    for offset, key_block, value_block, allowed in blocks:
        scores, grad_attn = block_terms(
            own_query, own_grad, key_block, value_block, allowed, score_scale
        )
        attention = jnp.exp(scores - log_total[:, :, None])
        attention_low = attention.astype(jnp.bfloat16)
        score_grad = (score_scale * attention * (grad_attn - row_delta[:, :, None])).astype(
            jnp.bfloat16
        )
        grad_query = grad_query + jnp.einsum(
            "hpq,qhe->phe", score_grad, key_block, preferred_element_type=jnp.float32
        )
        key_part = jnp.einsum(
            "hpq,phe->qhe", score_grad, own_query, preferred_element_type=jnp.float32
        ).astype(jnp.bfloat16)
        value_part = jnp.einsum(
            "hpq,phe->qhe", attention_low, own_grad, preferred_element_type=jnp.float32
        ).astype(jnp.bfloat16)
        part_pair = jnp.stack(
            [key_part.reshape(patches, feature_width), value_part.reshape(patches, feature_width)]
        )
        if offset == 0:
            arrived = part_pair
        elif offset > 0:
            arrived = passed_along(part_pair, "var", offset)
        else:
            arrived = passed_along(part_pair, "var", offset)
        summed = summed + arrived.astype(jnp.float32)
    grad_kv = summed.astype(jnp.bfloat16)
    grad_qkv = jnp.concatenate(
        [grad_query.astype(jnp.bfloat16).reshape(patches, feature_width), grad_kv[0], grad_kv[1]],
        axis=1,
    )
    input_grad = jnp.einsum(
        "pc,rc->pr",
        grad_qkv,
        lax.all_gather(proj_weight, "var", axis=1, tiled=True)[0],
        preferred_element_type=jnp.float32,
    )
    passed = passed_along(input_grad.astype(jnp.bfloat16), "segment", -1)
    return passed.reshape(1, 1, 1, patches, input_grad.shape[1])


def solution(mesh):
    return jax.shard_map(
        shards,
        mesh=mesh,
        in_specs=(
            P("dp", "segment", "var", None, None),
            P("dp", "segment", "var", None, None),
            P("dp", "segment", "var", None, None),
            P("dp", "segment", "var", None, None),
            P("segment", "var", None),
            P(),
        ),
        out_specs=P("dp", "segment", "var", None, None),
        check_vma=False,
    )
```

profile of v0, /device:TPU:88, one launch (start us, length us, event | category | flops | bytes accessed | tf_op | source)
XLA Modules:
  0.0 683.4 jit_solution(17258205993136301637)
XLA Ops:
  8.9 7.6 %collective-permute-start.7 = (bf16[2,256,1024]{2,1,0:T(8,128)(2,1)}, bf16[2,256,1024]{2,1,0:T(8,128)(2,1)}, u32[]{:S(2)}, u32[]{:S(2)}) collective-permute-start(bf16[2,256,1024]{2,1,0:T(8,128)(2,1)} %pad_maximum_fusion), channel_id=1, source_target_pairs={{32,0},{40,8},{48,16},{56,24},{64,32},{72,40},{80,48},{88,56},{96,... | collective-permute-start | bytes 3145736 | tf_op jit(solution)/shard_map/ppermute | solution.py:18
  16.5 7.6 %collective-permute-start.5 = (bf16[2,256,1024]{2,1,0:T(8,128)(2,1)}, bf16[2,256,1024]{2,1,0:T(8,128)(2,1)}, u32[]{:S(2)}, u32[]{:S(2)}) collective-permute-start(bf16[2,256,1024]{2,1,0:T(8,128)(2,1)} %pad_maximum_fusion), channel_id=1, source_target_pairs={{24,0},{32,8},{40,16},{48,24},{56,32},{64,40},{72,48},{80,56},{88,... | collective-permute-start | bytes 3145736 | tf_op jit(solution)/shard_map/ppermute | solution.py:18
  30.6 6.6 compare_and_fusion.8
  39.9 54.9 %collective-permute-done.7 = bf16[2,256,1024]{2,1,0:T(8,128)(2,1)} collective-permute-done((bf16[2,256,1024]{2,1,0:T(8,128)(2,1)}, bf16[2,256,1024]{2,1,0:T(8,128)(2,1)}, u32[]{:S(2)}, u32[]{:S(2)}) %collective-permute-start.7) | collective-permute-done | bytes 1048608 | tf_op jit(solution)/shard_map/ppermute | solution.py:18
  96.8 22.0 %collective-permute-done.6 = bf16[2,256,1024]{2,1,0:T(8,128)(2,1)} collective-permute-done((bf16[2,256,1024]{2,1,0:T(8,128)(2,1)}, bf16[2,256,1024]{2,1,0:T(8,128)(2,1)}, u32[]{:S(2)}, u32[]{:S(2)}) %collective-permute-start.6) | collective-permute-done | bytes 1048608 | tf_op jit(solution)/shard_map/ppermute | solution.py:18
  121.0 66.1 %collective-permute-done.5 = bf16[2,256,1024]{2,1,0:T(8,128)(2,1)} collective-permute-done((bf16[2,256,1024]{2,1,0:T(8,128)(2,1)}, bf16[2,256,1024]{2,1,0:T(8,128)(2,1)}, u32[]{:S(2)}, u32[]{:S(2)}) %collective-permute-start.5) | collective-permute-done | bytes 1048608 | tf_op jit(solution)/shard_map/ppermute | solution.py:18
  187.1 8.6 %collective-permute-start = (bf16[2,256,1024]{2,1,0:T(8,128)(2,1)}, bf16[2,256,1024]{2,1,0:T(8,128)(2,1)}, u32[]{:S(2)}, u32[]{:S(2)}) collective-permute-start(bf16[2,256,1024]{2,1,0:T(8,128)(2,1)} %pad_maximum_fusion), channel_id=1, source_target_pairs={{248,0},{0,8},{8,16},{16,24},{24,32},{32,40},{40,48},{48,56},{56,6... | collective-permute-start | bytes 3145736 | tf_op jit(solution)/shard_map/ppermute | solution.py:18
  203.2 51.2 %collective-permute-done.3 = bf16[2,256,1024]{2,1,0:T(8,128)(2,1)} collective-permute-done((bf16[2,256,1024]{2,1,0:T(8,128)(2,1)}, bf16[2,256,1024]{2,1,0:T(8,128)(2,1)}, u32[]{:S(2)}, u32[]{:S(2)}) %collective-permute-start.3) | collective-permute-done | bytes 1048608 | tf_op jit(solution)/shard_map/ppermute | solution.py:18
  257.5 6.0 collective-permute-done.2
  266.6 38.7 %collective-permute-done.1 = bf16[2,256,1024]{2,1,0:T(8,128)(2,1)} collective-permute-done((bf16[2,256,1024]{2,1,0:T(8,128)(2,1)}, bf16[2,256,1024]{2,1,0:T(8,128)(2,1)}, u32[]{:S(2)}, u32[]{:S(2)}) %collective-permute-start.1) | collective-permute-done | bytes 1048608 | tf_op jit(solution)/shard_map/ppermute | solution.py:18
  336.7 4.3 fusion.20
  341.1 3.8 fusion.17
  365.3 3.5 fusion.2
  369.5 19.8 %multiply_convert_fusion = (bf16[16,256,256]{1,2,0:T(8,128)(2,1)S(1)}, bf16[16,256,256]{1,2,0:T(8,128)(2,1)}, bf16[16,256,256]{1,2,0:T(8,128)(2,1)}, bf16[16,256,256]{1,2,0:T(8,128)(2,1)}, bf16[16,256,256]{1,2,0:T(8,128)(2,1)}) fusion(f32[16,256,256]{1,2,0:T(8,128)} %get-tuple-element.105, f32[16,256,256]{1,2,0:T(8,128)} %get-tuple-element.96, ...), kind=kLoop, calls=%fused_computation.58 | loop fusion | flops 36700160 | bytes 52789248 | tf_op jit(solution)/shard_map/convert_element_type | solution.py:90
  404.0 6.7 collective-permute-start.10
  413.8 15.2 %fusion.13 = (bf16[16,256,256]{1,2,0:T(8,128)(2,1)}, bf16[16,256,256]{1,2,0:T(8,128)(2,1)}, bf16[16,256,256]{1,2,0:T(8,128)(2,1)}, bf16[16,256,256]{1,2,0:T(8,128)(2,1)}) fusion(f32[16,256,256]{2,1,0:T(8,128)} %get-tuple-element.100, f32[16,256,256]{2,1,0:T(8,128)} %copy-done.8, f32[16,256]{1,0:T(8,128)S(1)} %copy-done.59, f32[16,256]{1,0:T(8,128)S(1)} %log_add_fusion, ...), kind=kLoop, calls=%fused_computation.21 | loop fusion | flops 29360128 | bytes 42237952 | tf_op jit(solution)/shard_map/convert_element_type | solution.py:90
  434.9 10.2 %collective-permute-start.12 = (bf16[2,256,1024]{1,2,0:T(8,128)(2,1)S(1)}, bf16[2,256,1024]{1,2,0:T(8,128)(2,1)S(1)}, u32[]{:S(2)}, u32[]{:S(2)}) collective-permute-start(bf16[2,256,1024]{1,2,0:T(8,128)(2,1)S(1)} %pad_maximum_fusion.5), channel_id=1, source_target_pairs={{24,0},{32,8},{40,16},{48,24},{56,32},{64,40},{72,48},{80,56},{88,... | collective-permute-start | bytes 3145736 | tf_op jit(solution)/shard_map/ppermute | solution.py:18
  459.1 3.9 collective-permute-start.14
  463.0 24.6 %collective-permute-done.10 = bf16[2,256,1024]{1,2,0:T(8,128)(2,1)} collective-permute-done((bf16[2,256,1024]{1,2,0:T(8,128)(2,1)}, bf16[2,256,1024]{1,2,0:T(8,128)(2,1)}, u32[]{:S(2)}, u32[]{:S(2)}) %collective-permute-start.10) | collective-permute-done | bytes 1048608 | tf_op jit(solution)/shard_map/ppermute | solution.py:18
  490.4 89.7 %collective-permute-done.12 = bf16[2,256,1024]{1,2,0:T(8,128)(2,1)S(1)} collective-permute-done((bf16[2,256,1024]{1,2,0:T(8,128)(2,1)S(1)}, bf16[2,256,1024]{1,2,0:T(8,128)(2,1)S(1)}, u32[]{:S(2)}, u32[]{:S(2)}) %collective-permute-start.12) | collective-permute-done | bytes 1048608 | tf_op jit(solution)/shard_map/ppermute | solution.py:18
  580.1 58.4 %collective-permute-done.13 = bf16[2,256,1024]{1,2,0:T(8,128)(2,1)S(1)} collective-permute-done((bf16[2,256,1024]{1,2,0:T(8,128)(2,1)S(1)}, bf16[2,256,1024]{1,2,0:T(8,128)(2,1)S(1)}, u32[]{:S(2)}, u32[]{:S(2)}) %collective-permute-start.13) | collective-permute-done | bytes 1048608 | tf_op jit(solution)/shard_map/ppermute | solution.py:18
  638.5 3.5 add_convert_fusion
  642.2 8.0 %fusion.44 = bf16[256,2048]{1,0:T(8,128)(2,1)S(1)} fusion(bf16[1,2048,3072]{2,1,0:T(8,128)(2,1)} %all-gather.2.cloned.1.call-done, bf16[256,1024]{0,1:T(8,128)(2,1)S(1)} %get-tuple-element.43, bf16[256,1024]{0,1:T(8,128)(2,1)S(1)} %get-tuple-element.42, bf16[256,1024]{0,1:T(8,128)(2,1)S(1)} %bitcast.471), kind=kOutput, calls=%fused_computation.89 | convolution fusion | flops 3226468352 | bytes 15204352 | tf_op jit(solution)/shard_map/pc,rc->pr/dot_general | solution.py:117
  651.3 23.8 %collective-permute-done.16 = bf16[256,2048]{1,0:T(8,128)(2,1)S(1)} collective-permute-done((bf16[256,2048]{1,0:T(8,128)(2,1)S(1)}, bf16[256,2048]{1,0:T(8,128)(2,1)S(1)}, u32[]{:S(2)}, u32[]{:S(2)}) %collective-permute-start.16) | collective-permute-done | bytes 1048608 | tf_op jit(solution)/shard_map/ppermute | solution.py:18
  (229 shorter events, 123.9 us)
Async XLA Ops:
  6.5 635.6 %all-gather.2.cloned.1.call-start = ((), (), s32[]{:S(2)}) async-start(), calls=%async_computation | async-start | bytes 12976128 | tf_op jit(solution)/shard_map/all_gather | solution.py:120
  8.9 85.9 %collective-permute-start.7 = (bf16[2,256,1024]{2,1,0:T(8,128)(2,1)}, bf16[2,256,1024]{2,1,0:T(8,128)(2,1)}, u32[]{:S(2)}, u32[]{:S(2)}) collective-permute-start(bf16[2,256,1024]{2,1,0:T(8,128)(2,1)} %pad_maximum_fusion), channel_id=1, source_target_pairs={{32,0},{40,8},{48,16},{56,24},{64,32},{72,40},{80,48},{88,56},{96,... | collective-permute-start | bytes 3145736 | tf_op jit(solution)/shard_map/ppermute | solution.py:18
  16.5 102.3 %collective-permute-start.6 = (bf16[2,256,1024]{2,1,0:T(8,128)(2,1)}, bf16[2,256,1024]{2,1,0:T(8,128)(2,1)}, u32[]{:S(2)}, u32[]{:S(2)}) collective-permute-start(bf16[2,256,1024]{2,1,0:T(8,128)(2,1)} %pad_maximum_fusion), channel_id=1, source_target_pairs={{224,0},{232,8},{240,16},{248,24},{0,32},{8,40},{16,48},{24,56},{3... | collective-permute-start | bytes 3145736 | tf_op jit(solution)/shard_map/ppermute | solution.py:18
  16.5 170.6 %collective-permute-start.5 = (bf16[2,256,1024]{2,1,0:T(8,128)(2,1)}, bf16[2,256,1024]{2,1,0:T(8,128)(2,1)}, u32[]{:S(2)}, u32[]{:S(2)}) collective-permute-start(bf16[2,256,1024]{2,1,0:T(8,128)(2,1)} %pad_maximum_fusion), channel_id=1, source_target_pairs={{24,0},{32,8},{40,16},{48,24},{56,32},{64,40},{72,48},{80,56},{88,... | collective-permute-start | bytes 3145736 | tf_op jit(solution)/shard_map/ppermute | solution.py:18
  24.1 173.8 %collective-permute-start.4 = (bf16[2,256,1024]{2,1,0:T(8,128)(2,1)}, bf16[2,256,1024]{2,1,0:T(8,128)(2,1)S(1)}, u32[]{:S(2)}, u32[]{:S(2)}) collective-permute-start(bf16[2,256,1024]{2,1,0:T(8,128)(2,1)} %pad_maximum_fusion), channel_id=1, source_target_pairs={{232,0},{240,8},{248,16},{0,24},{8,32},{16,40},{24,48},{32,56},{40... | collective-permute-start | bytes 3145736 | tf_op jit(solution)/shard_map/ppermute | solution.py:18
  24.1 230.3 %collective-permute-start.3 = (bf16[2,256,1024]{2,1,0:T(8,128)(2,1)}, bf16[2,256,1024]{2,1,0:T(8,128)(2,1)}, u32[]{:S(2)}, u32[]{:S(2)}) collective-permute-start(bf16[2,256,1024]{2,1,0:T(8,128)(2,1)} %pad_maximum_fusion), channel_id=1, source_target_pairs={{16,0},{24,8},{32,16},{40,24},{48,32},{56,40},{64,48},{72,56},{80,... | collective-permute-start | bytes 3145736 | tf_op jit(solution)/shard_map/ppermute | solution.py:18
  94.8 168.8 %collective-permute-start.2 = (bf16[2,256,1024]{2,1,0:T(8,128)(2,1)}, bf16[2,256,1024]{2,1,0:T(8,128)(2,1)}, u32[]{:S(2)}, u32[]{:S(2)}) collective-permute-start(bf16[2,256,1024]{2,1,0:T(8,128)(2,1)} %pad_maximum_fusion), channel_id=1, source_target_pairs={{240,0},{248,8},{0,16},{8,24},{16,32},{24,40},{32,48},{40,56},{48,... | collective-permute-start | bytes 3145736 | tf_op jit(solution)/shard_map/ppermute | solution.py:18
  118.8 186.6 %collective-permute-start.1 = (bf16[2,256,1024]{2,1,0:T(8,128)(2,1)}, bf16[2,256,1024]{2,1,0:T(8,128)(2,1)}, u32[]{:S(2)}, u32[]{:S(2)}) collective-permute-start(bf16[2,256,1024]{2,1,0:T(8,128)(2,1)} %pad_maximum_fusion), channel_id=1, source_target_pairs={{8,0},{16,8},{24,16},{32,24},{40,32},{48,40},{56,48},{64,56},{72,6... | collective-permute-start | bytes 3145736 | tf_op jit(solution)/shard_map/ppermute | solution.py:18
  187.1 121.4 %collective-permute-start = (bf16[2,256,1024]{2,1,0:T(8,128)(2,1)}, bf16[2,256,1024]{2,1,0:T(8,128)(2,1)}, u32[]{:S(2)}, u32[]{:S(2)}) collective-permute-start(bf16[2,256,1024]{2,1,0:T(8,128)(2,1)} %pad_maximum_fusion), channel_id=1, source_target_pairs={{248,0},{0,8},{8,16},{16,24},{24,32},{32,40},{40,48},{48,56},{56,6... | collective-permute-start | bytes 3145736 | tf_op jit(solution)/shard_map/ppermute | solution.py:18
  200.3 130.2 %copy-start.34 = (bf16[1,256,1024]{1,2,0:T(8,128)(2,1)}, bf16[1,256,1024]{1,2,0:T(8,128)(2,1)S(1)}, u32[]{:S(2)}) copy-start(bf16[1,256,1024]{1,2,0:T(8,128)(2,1)S(1)} %copy.111) | copy-start | bytes 1572868
  201.7 129.6 %copy-start.32 = (bf16[1,256,1024]{1,2,0:T(8,128)(2,1)}, bf16[1,256,1024]{1,2,0:T(8,128)(2,1)S(1)}, u32[]{:S(2)}) copy-start(bf16[1,256,1024]{1,2,0:T(8,128)(2,1)S(1)} %copy.109) | copy-start | bytes 1572868
  203.2 129.0 %copy-start.30 = (bf16[1,256,1024]{1,2,0:T(8,128)(2,1)}, bf16[1,256,1024]{1,2,0:T(8,128)(2,1)S(1)}, u32[]{:S(2)}) copy-start(bf16[1,256,1024]{1,2,0:T(8,128)(2,1)S(1)} %copy.107) | copy-start | bytes 1572868
  330.4 34.9 %copy-start.2 = (f32[16,256,256]{2,1,0:T(8,128)}, f32[16,256,256]{2,1,0:T(8,128)S(1)}, u32[]{:S(2)}) copy-start(f32[16,256,256]{2,1,0:T(8,128)S(1)} %get-tuple-element.80) | copy-start | bytes 12582916
  396.1 62.7 %collective-permute-start.8 = (bf16[2,256,1024]{1,2,0:T(8,128)(2,1)}, bf16[2,256,1024]{1,2,0:T(8,128)(2,1)}, u32[]{:S(2)}, u32[]{:S(2)}) collective-permute-start(bf16[2,256,1024]{1,2,0:T(8,128)(2,1)} %pad_maximum_fusion.1), channel_id=1, source_target_pairs={{8,0},{16,8},{24,16},{32,24},{40,32},{48,40},{56,48},{64,56},{72,6... | collective-permute-start | bytes 3145736 | tf_op jit(solution)/shard_map/ppermute | solution.py:18
  399.7 59.4 %collective-permute-start.9 = (bf16[2,256,1024]{1,2,0:T(8,128)(2,1)}, bf16[2,256,1024]{1,2,0:T(8,128)(2,1)}, u32[]{:S(2)}, u32[]{:S(2)}) collective-permute-start(bf16[2,256,1024]{1,2,0:T(8,128)(2,1)} %pad_maximum_fusion.2), channel_id=1, source_target_pairs={{248,0},{0,8},{8,16},{16,24},{24,32},{32,40},{40,48},{48,56},{56,6... | collective-permute-start | bytes 3145736 | tf_op jit(solution)/shard_map/ppermute | solution.py:18
  404.0 83.6 %collective-permute-start.10 = (bf16[2,256,1024]{1,2,0:T(8,128)(2,1)}, bf16[2,256,1024]{1,2,0:T(8,128)(2,1)}, u32[]{:S(2)}, u32[]{:S(2)}) collective-permute-start(bf16[2,256,1024]{1,2,0:T(8,128)(2,1)} %pad_maximum_fusion.3), channel_id=1, source_target_pairs={{16,0},{24,8},{32,16},{40,24},{48,32},{56,40},{64,48},{72,56},{80,... | collective-permute-start | bytes 3145736 | tf_op jit(solution)/shard_map/ppermute | solution.py:18
  413.6 76.8 %collective-permute-start.11 = (bf16[2,256,1024]{1,2,0:T(8,128)(2,1)}, bf16[2,256,1024]{1,2,0:T(8,128)(2,1)}, u32[]{:S(2)}, u32[]{:S(2)}) collective-permute-start(bf16[2,256,1024]{1,2,0:T(8,128)(2,1)} %pad_maximum_fusion.4), channel_id=1, source_target_pairs={{240,0},{248,8},{0,16},{8,24},{16,32},{24,40},{32,48},{40,56},{48,... | collective-permute-start | bytes 3145736 | tf_op jit(solution)/shard_map/ppermute | solution.py:18
  434.9 145.2 %collective-permute-start.12 = (bf16[2,256,1024]{1,2,0:T(8,128)(2,1)S(1)}, bf16[2,256,1024]{1,2,0:T(8,128)(2,1)S(1)}, u32[]{:S(2)}, u32[]{:S(2)}) collective-permute-start(bf16[2,256,1024]{1,2,0:T(8,128)(2,1)S(1)} %pad_maximum_fusion.5), channel_id=1, source_target_pairs={{24,0},{32,8},{40,16},{48,24},{56,32},{64,40},{72,48},{80,56},{88,... | collective-permute-start | bytes 3145736 | tf_op jit(solution)/shard_map/ppermute | solution.py:18
  458.7 30.7 %copy-start.25 = (bf16[16,256,256]{1,2,0:T(8,128)(2,1)S(1)}, bf16[16,256,256]{1,2,0:T(8,128)(2,1)}, u32[]{:S(2)}) copy-start(bf16[16,256,256]{1,2,0:T(8,128)(2,1)} %get-tuple-element.61) | copy-start | bytes 6291460
  458.7 30.7 %copy-start.29 = (bf16[1,256,1024]{1,2,0:T(8,128)(2,1)S(1)}, bf16[1,256,1024]{1,2,0:T(8,128)(2,1)}, u32[]{:S(2)}) copy-start(bf16[1,256,1024]{1,2,0:T(8,128)(2,1)} %copy-done.28) | copy-start | bytes 1572868
  458.7 179.8 %collective-permute-start.13 = (bf16[2,256,1024]{1,2,0:T(8,128)(2,1)S(1)}, bf16[2,256,1024]{1,2,0:T(8,128)(2,1)S(1)}, u32[]{:S(2)}, u32[]{:S(2)}) collective-permute-start(bf16[2,256,1024]{1,2,0:T(8,128)(2,1)S(1)} %pad_maximum_fusion.6), channel_id=1, source_target_pairs={{232,0},{240,8},{248,16},{0,24},{8,32},{16,40},{24,48},{32,56},{40... | collective-permute-start | bytes 3145736 | tf_op jit(solution)/shard_map/ppermute | solution.py:18
  459.1 179.4 %collective-permute-start.14 = (bf16[2,256,1024]{1,2,0:T(8,128)(2,1)S(1)}, bf16[2,256,1024]{1,2,0:T(8,128)(2,1)S(1)}, u32[]{:S(2)}, u32[]{:S(2)}) collective-permute-start(bf16[2,256,1024]{1,2,0:T(8,128)(2,1)S(1)} %pad_maximum_fusion.7), channel_id=1, source_target_pairs={{32,0},{40,8},{48,16},{56,24},{64,32},{72,40},{80,48},{88,56},{96,... | collective-permute-start | bytes 3145736 | tf_op jit(solution)/shard_map/ppermute | solution.py:18
  487.6 150.9 %collective-permute-start.15 = (bf16[2,256,1024]{1,2,0:T(8,128)(2,1)S(1)}, bf16[2,256,1024]{1,2,0:T(8,128)(2,1)S(1)}, u32[]{:S(2)}, u32[]{:S(2)}) collective-permute-start(bf16[2,256,1024]{1,2,0:T(8,128)(2,1)S(1)} %pad_maximum_fusion.8), channel_id=1, source_target_pairs={{224,0},{232,8},{240,16},{248,24},{0,32},{8,40},{16,48},{24,56},{3... | collective-permute-start | bytes 3145736 | tf_op jit(solution)/shard_map/ppermute | solution.py:18
  650.2 25.0 %collective-permute-start.16 = (bf16[256,2048]{1,0:T(8,128)(2,1)S(1)}, bf16[256,2048]{1,0:T(8,128)(2,1)S(1)}, u32[]{:S(2)}, u32[]{:S(2)}) collective-permute-start(bf16[256,2048]{1,0:T(8,128)(2,1)S(1)} %fusion.44), channel_id=1, source_target_pairs={{1,0},{2,1},{3,2},{0,3},{5,4},{6,5},{7,6},{4,7},{9,8},{10,9},{11,1... | collective-permute-start | bytes 3145736 | tf_op jit(solution)/shard_map/ppermute | solution.py:18
  (55 other events, 376.5 us)
Sparse Core Ops, SparseCore 0:
  25.7 291.4 all-gather.1
where the time goes:
time: 691 us; the launch traced here: 683 us
  waiting for transfers between devices  435 us (63%)
  matrix products  79.6 us (12%)
  other arithmetic  53.7 us (8%)
  local copies, waits for them, and re-layouts  50.6 us (7%)
  starting transfers between devices  49.2 us (7%)
  between operations  14.9 us (2%)
    ppermute x17, waiting for transfers between devices, passed_along(): return lax.ppermute(block, axis, route)  435 us
    ppermute x17, starting transfers between devices, passed_along(): return lax.ppermute(block, axis, route)  49.2 us
    convert_element_type x2, other arithmetic, shards(): (score_scale * attention * (grad_attn - row_delta[:, :, None])).astype(jn...  35 us
    slice x16, local copies, waits for them, and re-layouts, shards(): pair_block[1].reshape(token_shape)  32.6 us
    dot_general x9, matrix products, block_terms(): jnp.einsum('phe,qhe->hpq', own_grad, value_block, preferred_element_type=...  32 us
    dot_general x9, matrix products, shards(): jnp.einsum('hpq,phe->qhe', attention_low, own_grad, preferred_element_typ...  14.2 us
  transfers between devices with their start and end apart: 18, of which 10 were waited for; matrix products, arithmetic and copies ran while one was open for 25% of the time, Pallas kernels for 0%

commit v1 on v0

v1 whole, which is shorter than its diff:
```python
import functools
import math

import jax
import jax.numpy as jnp
from jax import lax
from jax.experimental import pallas as pl
from jax.experimental.pallas import tpu as pltpu
from jax.sharding import PartitionSpec as P

HEAD = 64
CAUSAL = 128
ROW = 8
REACH = 4
SLOTS = ROW + 2 * REACH
WINDOW = 2 * REACH + 1
PATCHES = 256
LANES = 128
MESH = pl.DeviceIdType.MESH
F32 = jnp.float32
BF16 = jnp.bfloat16
ARRIVAL = (0, 1, 7, 2, 6, 3, 5, 4)


def mod(a, n):
    return lax.rem(a + 4 * n, n)


def dot(a, b, ca, cb):
    return lax.dot_general(a, b, (((ca,), (cb,)), ((), ())), preferred_element_type=F32)


def two_heads(block, scale=None):
    if scale is not None:
        block = block * jnp.asarray(scale, block.dtype)
    first = lax.broadcasted_iota(jnp.int32, block.shape, 1) < HEAD
    zero = jnp.zeros_like(block)
    return jnp.concatenate([jnp.where(first, block, zero), jnp.where(first, zero, block)], axis=0)


def first_pass(v, refs):
    kbuf, vbuf, kT, qbuf, obuf, qc, oc, p_s, a_s, st, dkacc, dvacc, dqout = refs
    for g in range(2):
        rows = pl.ds(g * CAUSAL, CAUSAL)
        qc[g] = two_heads(qbuf[v, rows, :], 0.125)
        oc[g] = two_heads(obuf[v, rows, :])

    def one(w):
        slot = v + w
        for g in range(2):
            n = CAUSAL * (g + 1)
            s = dot(kbuf[slot, 0:n, :], qc[g], 1, 1)
            m = jnp.max(s, axis=0, keepdims=True)
            p = jnp.exp(s - m)
            a = dot(vbuf[slot, 0:n, :], oc[g], 1, 1)
            at = pl.ds(g * CAUSAL, n)
            p_s[w, at, :] = p
            a_s[w, at, :] = a
            st[0, w, g : g + 1, :] = m
            st[1, w, g : g + 1, :] = jnp.sum(p, axis=0, keepdims=True)
            st[2, w, g : g + 1, :] = jnp.sum(p * a, axis=0, keepdims=True)

    for w in range(WINDOW):
        one(w)


def second_pass(v, linked, refs):
    kbuf, vbuf, kT, qbuf, obuf, qc, oc, p_s, a_s, st, dkacc, dvacc, dqout = refs
    top = jnp.full((2, 256), -1e30, F32)
    for w in range(WINDOW):
        top = jnp.maximum(top, jnp.where(linked[w], st[0, w, 0:2, :], -1e30))
    total = jnp.zeros((2, 256), F32)
    weighted = jnp.zeros((2, 256), F32)
    for w in range(WINDOW):
        f = jnp.where(linked[w], jnp.exp(jnp.minimum(st[0, w, 0:2, :] - top, 0.0)), 0.0)
        total += f * st[1, w, 0:2, :]
        weighted += f * st[2, w, 0:2, :]
        st[0, w, 0:2, :] = f
    share = 1.0 / total
    delta = weighted * share
    st[3, 0, 0:2, :] = share
    st[3, 1, 0:2, :] = delta

    def one(w, sums):
        slot = v + w
        out = []
        parts = []
        for g in range(2):
            n = CAUSAL * (g + 1)
            at = pl.ds(g * CAUSAL, n)
            f = st[0, w, g : g + 1, :] * st[3, 0, g : g + 1, :]
            attention = p_s[w, at, :] * f
            ds = (attention * (a_s[w, at, :] - st[3, 1, g : g + 1, :])).astype(BF16)
            low = attention.astype(BF16)
            out.append(sums[g] + dot(kT[slot, :, 0:n], ds, 1, 0))
            parts.append((dot(ds, qc[g], 1, 0), dot(low, oc[g], 1, 0)))
        dkacc[slot, 0:CAUSAL, :] += parts[0][0] + parts[1][0][0:CAUSAL]
        dkacc[slot, CAUSAL:, :] += parts[1][0][CAUSAL:]
        dvacc[slot, 0:CAUSAL, :] += parts[0][1] + parts[1][1][0:CAUSAL]
        dvacc[slot, CAUSAL:, :] += parts[1][1][CAUSAL:]
        return out

    sums = [jnp.zeros((LANES, 256), F32)] * 2
    for w in range(WINDOW):
        sums = one(w, sums)
    for g in range(2):
        both = jnp.concatenate([sums[g][0:HEAD, 0:CAUSAL], sums[g][HEAD:, CAUSAL:]], axis=0)
        dqout[v, pl.ds(g * CAUSAL, CAUSAL), :] = (both.T * 0.125).astype(BF16)


def linked_row(links, gv, var_count):
    entries = [links[gv, j] for j in range(WINDOW)]
    linked = []
    for w in range(WINDOW):
        target = mod(gv + w - REACH, var_count)
        hit = entries[0] == target
        for e in entries[1:]:
            hit = jnp.logical_or(hit, e == target)
        linked.append(hit)
    return linked


def ring_order(j):
    half = (j + 1) // 2
    return REACH + half * (1 - 2 * lax.rem(j, 2))


def kernel(var_count, segments, rows_of_x, links, q_in, k_in, v_in, o_in, w_in, out,
           kbuf, vbuf, kT, qbuf, obuf, qc, oc, p_s, a_s, st, dkacc, dvacc, dqout,
           kvout, back, grads, wbuf,
           in_send, in_recv, own_sem, halo_send, halo_recv, dq_send, dq_recv,
           back_send, back_recv, kv_send, kv_recv,
           wy_send, wy_recv, wz_send, wz_recv, wx_send, wx_recv, wf_send, wf_recv, wc_send, wc_recv):
    me = lax.axis_index("var")
    core = lax.axis_index("dp")
    seg = lax.axis_index("segment")
    x, z = me // ROW, lax.rem(me, ROW)
    seg_down = mod(seg - 1, segments)
    seg_up = mod(seg + 1, segments)

    def at(xx, zz):
        return {"var": mod(xx, rows_of_x) * ROW + mod(zz, ROW)}

    def at_down(zz):
        return {"var": x * ROW + mod(zz, ROW), "segment": seg_down}

    barrier = pltpu.get_barrier_semaphore()

    def greet(where):
        pl.semaphore_signal(barrier, inc=1, device_id=where, device_id_type=MESH)

    def greet_z(d, _):
        greet(at(x, z + d))
        return 0

    def greet_y(d, _):
        greet({"var": x * ROW + mod(z + d, ROW), "segment": seg_down})
        greet({"var": x * ROW + mod(z + d, ROW), "segment": seg_up})
        return 0

    lax.fori_loop(1, ROW, greet_z, 0)
    greet(at(x + 1, z))
    greet(at(x - 1, z))
    greet({"dp": 1 - core})
    lax.fori_loop(0, ROW, greet_y, 0)
    pl.semaphore_wait(barrier, (ROW - 1) + 3 + 2 * ROW)

    def remote(src, dst, send, recv, where):
        return pltpu.make_async_remote_copy(
            src_ref=src, dst_ref=dst, send_sem=send, recv_sem=recv, device_id=where, device_id_type=MESH
        )

    def w_down():
        return remote(w_in.at[core], wbuf.at[me, core], wy_send, wy_recv, {"segment": seg_down})

    def w_var(xx, r):
        return mod(xx, rows_of_x) * ROW + mod(z - r, ROW)

    def w_z(r, step):
        ref = wbuf.at[w_var(x, r), core]
        there = (r + step) % ROW
        return remote(ref, ref, wz_send.at[there], wz_recv.at[there], at(x, z + step))

    def w_x(r, step):
        ref = wbuf.at[w_var(x, r), core]
        side = (step + 1) // 2
        return remote(ref, ref, wx_send.at[side, r], wx_recv.at[side, r], at(x + step, z))

    def w_f(r, step):
        ref = wbuf.at[w_var(x - step, r), core]
        return remote(ref, ref, wf_send.at[r], wf_recv.at[r], at(x + step, z))

    def w_c(xs, r):
        ref = wbuf.at[w_var(x + xs, r), core]
        return remote(ref, ref, wc_send.at[xs, r], wc_recv.at[xs, r], {"dp": 1 - core})

    def w_c_arrives(xs, r):
        ref = wbuf.at[w_var(x + xs, r), 1 - core]
        return remote(ref, ref, wc_send.at[xs, r], wc_recv.at[xs, r], {"dp": 1 - core})

    def w_spread(r):
        w_x(r, 1).start()
        w_x(r, -1).start()
        w_c(0, r).start()

    def w_own():
        w_down().wait_recv()
        w_z(0, 1).start()
        w_z(0, -1).start()
        w_spread(0)

    def w_z_arrived(r):
        ref = wbuf.at[w_var(x, r), core]
        remote(ref, ref, wz_send.at[r], wz_recv.at[r], at(x, z + 1)).wait_recv()
        if r in (1, 2, 3):
            w_z(r, 1).start()
        if r in (7, 6):
            w_z(r, -1).start()
        w_spread(r)

    def w_x_arrived(r):
        for step in (1, -1):
            ref = wbuf.at[w_var(x - step, r), core]
            side = (step + 1) // 2
            remote(ref, ref, wx_send.at[side, r], wx_recv.at[side, r], at(x + step, z)).wait_recv()
            if (r % 2 == 0) == (step == 1):
                w_f(r, step).start()
            w_c((-step) % 4, r).start()

    def w_f_arrived(r):
        ref = wbuf.at[w_var(x + 2, r), core]
        remote(ref, ref, wf_send.at[r], wf_recv.at[r], at(x + 1, z)).wait_recv()
        w_c(2, r).start()

    w_down().start()

    def columns(zz):
        return pl.ds(pl.multiple_of(zz * LANES, LANES), LANES)

    ins = ((k_in, kbuf, REACH), (v_in, vbuf, REACH), (q_in, qbuf, 0), (o_in, obuf, 0))

    def own(kind):
        src, dst, first = ins[kind]
        return pltpu.make_async_copy(src.at[:, columns(z)], dst.at[first + z], own_sem.at[kind])

    def to_peer(kind, d):
        src, dst, first = ins[kind]
        return remote(src.at[:, columns(mod(z + d, ROW))], dst.at[first + z],
                      in_send.at[kind, d], in_recv.at[kind, d], at(x, z + d))

    def from_peer(kind, d):
        src, dst, first = ins[kind]
        return remote(src.at[:, columns(z)], dst.at[first + mod(z - d, ROW)],
                      in_send.at[kind, d], in_recv.at[kind, d], at(x, z + d))

    for kind in range(4):
        own(kind).start()

    def send_kv(j, _):
        d = ring_order(j)
        to_peer(0, d).start()
        to_peer(1, d).start()
        return 0

    def send_qo(j, _):
        d = ring_order(6 - j)
        to_peer(2, d).start()
        to_peer(3, d).start()
        return 0

    lax.fori_loop(0, ROW - 1, send_kv, 0)
    lax.fori_loop(0, ROW - 1, send_qo, 0)
    w_own()

    def halo(kind, zs):
        buf = (kbuf, vbuf)[kind]
        up = zs // REACH
        return remote(buf.at[REACH + zs], buf.at[lax.rem(zs + 12, SLOTS)],
                      halo_send.at[kind, zs], halo_recv.at[kind, zs], at(x + 2 * up - 1, z))

    for kind in range(2):
        own(kind).wait()
        halo(kind, z).start()

    dkacc[...] = jnp.zeros_like(dkacc)
    dvacc[...] = jnp.zeros_like(dvacc)

    def take_kv(j, _):
        d = ring_order(6 - j)
        zs = mod(z - d, ROW)
        for kind in range(2):
            from_peer(kind, d).wait_recv()
            halo(kind, zs).start()
        return 0

    lax.fori_loop(0, ROW - 1, take_kv, 0)

    def turn(slot):
        kT[slot] = kbuf[slot].T

    def turn_own(j, _):
        turn(REACH + j)
        return 0

    lax.fori_loop(0, ROW, turn_own, 0)

    def take_halo(zs, _):
        slot = lax.rem(zs + 12, SLOTS)
        for kind in range(2):
            buf = (kbuf, vbuf)[kind]
            remote(buf.at[REACH + zs], buf.at[slot], halo_send.at[kind, zs], halo_recv.at[kind, zs],
                   at(x + 1, z)).wait_recv()
        turn(slot)
        return 0

    lax.fori_loop(0, ROW, take_halo, 0)
    own(2).wait()
    own(3).wait()

    refs = (kbuf, vbuf, kT, qbuf, obuf, qc, oc, p_s, a_s, st, dkacc, dvacc, dqout)

    def dq_home(d):
        return remote(dqout.at[mod(z - d, ROW)], grads.at[:, columns(z)],
                      dq_send.at[d], dq_recv.at[d], at_down(z - d))

    def step(j, _):
        d = ring_order(7 - j)
        v = mod(z - d, ROW)

        @pl.when(j > 0)
        def _():
            from_peer(2, d).wait_recv()
            from_peer(3, d).wait_recv()

        first_pass(v, refs)

        @pl.when(j > 0)
        def _():
            dq_home(ring_order(8 - j)).start()

        for when, work in {2: (1, 7), 3: (2, 6), 4: (3, 5), 5: (4,)}.items():
            @pl.when(j == when)
            def _(work=work):
                for r in work:
                    w_z_arrived(r)

        for when, work in {3: (0,), 5: (1,), 6: (7,), 7: (2,)}.items():
            @pl.when(j == when)
            def _(work=work):
                for r in work:
                    w_x_arrived(r)

        second_pass(v, linked_row(links, x * ROW + v, var_count), refs)
        return 0

    lax.fori_loop(0, ROW, step, 0)

    def out_halo(j):
        return j + ROW * (j // REACH)

    def cast_halo(j, _):
        slot = out_halo(j)
        kvout[0, slot] = dkacc[slot].astype(BF16)
        kvout[1, slot] = dvacc[slot].astype(BF16)
        return 0

    def send_back(kind, j):
        slot = out_halo(j)
        zs = lax.rem(slot + 4, SLOTS)
        up = j // REACH
        return remote(kvout.at[kind, slot], back.at[kind, zs], back_send.at[kind, zs], back_recv.at[kind, zs],
                      at(x + 2 * up - 1, z))

    lax.fori_loop(0, ROW, cast_halo, 0)

    def start_back(j, _):
        send_back(0, j).start()
        send_back(1, j).start()
        return 0

    lax.fori_loop(0, ROW, start_back, 0)
    dq_home(REACH).start()
    w_x_arrived(6)
    w_f_arrived(0)

    def from_back(kind, zs):
        return remote(kvout.at[kind, 0], back.at[kind, zs], back_send.at[kind, zs], back_recv.at[kind, zs],
                      at(x + 1, z))

    def kv_home(kind, d):
        zs = mod(z - d, ROW)
        col = pl.ds(pl.multiple_of((kind + 1) * ROW * LANES + z * LANES, LANES), LANES)
        return remote(kvout.at[kind, REACH + zs], grads.at[:, col],
                      kv_send.at[kind, d], kv_recv.at[kind, d], at_down(zs))

    def total(d):
        zs = mod(z - d, ROW)
        for kind in range(2):
            from_back(kind, zs).wait_recv()
            acc = (dkacc, dvacc)[kind]
            kvout[kind, REACH + zs] = (acc[REACH + zs] + back[kind, zs].astype(F32)).astype(BF16)

    def send_home(j, _):
        total(ring_order(j))

        @pl.when(j > 0)
        def _():
            kv_home(0, ring_order(j - 1)).start()
            kv_home(1, ring_order(j - 1)).start()

        return 0

    lax.fori_loop(0, ROW, send_home, 0)
    for r in (3, 5, 4):
        w_x_arrived(r)
        if r == 3:
            kv_home(0, 0).start()
            kv_home(1, 0).start()
    for r in ARRIVAL[1:]:
        w_f_arrived(r)

    for r in range(ROW):
        for xs in range(4):
            w_c_arrives(xs, r).wait_recv()

    def grads_arrive(d, _):
        zs = mod(z + d, ROW)
        remote(dqout.at[0], grads.at[:, columns(zs)], dq_send.at[d], dq_recv.at[d], at_down(z)).wait_recv()
        for kind in range(2):
            col = pl.ds(pl.multiple_of((kind + 1) * ROW * LANES + zs * LANES, LANES), LANES)
            remote(kvout.at[kind, 0], grads.at[:, col], kv_send.at[kind, d], kv_recv.at[kind, d],
                   at_down(z)).wait_recv()
        return 0

    lax.fori_loop(0, ROW, grads_arrive, 0)

    chunk = 4

    def project(c, _):
        w = wbuf[pl.ds(c * chunk, chunk)].reshape(chunk * 64, wbuf.shape[3])
        cols = pl.ds(pl.multiple_of(c * chunk * 64, chunk * 64), chunk * 64)
        out[:, cols] = dot(grads[...], w, 1, 1).astype(BF16)
        return 0

    lax.fori_loop(0, wbuf.shape[0] // chunk, project, 0)

    def left_z(d, _):
        for kind in range(4):
            to_peer(kind, d).wait_send()
        return 0

    lax.fori_loop(1, ROW, left_z, 0)

    def left(d, _):
        dq_home(d).wait_send()
        for kind in range(2):
            halo(kind, d).wait_send()
            kv_home(kind, d).wait_send()
            send_back(kind, d).wait_send()
        return 0

    lax.fori_loop(0, ROW, left, 0)
    w_down().wait_send()
    for r in range(ROW):
        if r in (0, 1, 2, 3):
            w_z(r, 1).wait_send()
        if r in (0, 7, 6):
            w_z(r, -1).wait_send()
        w_x(r, 1).wait_send()
        w_x(r, -1).wait_send()
        w_f(r, 1 if r % 2 == 0 else -1).wait_send()
        for xs in range(4):
            w_c(xs, r).wait_send()


def shards(queries, keys, values, out_grad, proj_weight, links):
    patches, width = queries.shape[3], queries.shape[4]
    rows, cols = proj_weight.shape[1], proj_weight.shape[2]
    var_count = lax.axis_size("var")
    segments = lax.axis_size("segment")
    rows_of_x = var_count // ROW
    dma = pltpu.SemaphoreType.DMA
    block = (PATCHES, LANES)
    passed = pl.pallas_call(
        functools.partial(kernel, var_count, segments, rows_of_x),
        out_shape=jax.ShapeDtypeStruct((patches, var_count * rows), BF16),
        in_specs=[pl.BlockSpec(memory_space=pltpu.SMEM)] + [pl.BlockSpec(memory_space=pl.ANY)] * 5,
        out_specs=pl.BlockSpec(memory_space=pltpu.VMEM),
        scratch_shapes=[
            pltpu.VMEM((SLOTS,) + block, BF16),
            pltpu.VMEM((SLOTS,) + block, BF16),
            pltpu.VMEM((SLOTS, LANES, PATCHES), BF16),
            pltpu.VMEM((ROW,) + block, BF16),
            pltpu.VMEM((ROW,) + block, BF16),
            pltpu.VMEM((2, 256, LANES), BF16),
            pltpu.VMEM((2, 256, LANES), BF16),
            pltpu.VMEM((WINDOW, 384, 256), F32),
            pltpu.VMEM((WINDOW, 384, 256), F32),
            pltpu.VMEM((4, WINDOW, 8, 256), F32),
            pltpu.VMEM((SLOTS,) + block, F32),
            pltpu.VMEM((SLOTS,) + block, F32),
            pltpu.VMEM((ROW,) + block, BF16),
            pltpu.VMEM((2, SLOTS) + block, BF16),
            pltpu.VMEM((2, ROW) + block, BF16),
            pltpu.VMEM((patches, cols), BF16),
            pltpu.VMEM((var_count, 2, rows // 2, cols), BF16),
            dma((4, ROW)), dma((4, ROW)), dma((4,)), dma((2, ROW)), dma((2, ROW)), dma((ROW,)), dma((ROW,)),
            dma((2, ROW)), dma((2, ROW)), dma((2, ROW)), dma((2, ROW)),
            dma(()), dma(()), dma((ROW,)), dma((ROW,)), dma((2, ROW)), dma((2, ROW)),
            dma((ROW,)), dma((ROW,)), dma((4, ROW)), dma((4, ROW)),
        ],
        compiler_params=pltpu.CompilerParams(
            collective_id=0, has_side_effects=True, vmem_limit_bytes=60 * 1024 * 1024
        ),
    )(
        links,
        queries.reshape(patches, width),
        keys.reshape(patches, width),
        values.reshape(patches, width),
        out_grad.reshape(patches, width),
        proj_weight.reshape(2, rows // 2, cols),
    )
    return passed.reshape(1, 1, 1, patches, var_count * rows)


def solution(mesh):
    return jax.shard_map(
        shards,
        mesh=mesh,
        in_specs=(
            P("dp", "segment", "var", None, None),
            P("dp", "segment", "var", None, None),
            P("dp", "segment", "var", None, None),
            P("dp", "segment", "var", None, None),
            P("segment", "var", None),
            P(),
        ),
        out_specs=P("dp", "segment", "var", None, None),
        check_vma=False,
    )
```

time: 691 us -> 149 us (0.22)
  waiting for transfers between devices: 435 us -> 0 us
  Pallas kernels: 0 us -> 143 us
  matrix products: 79.6 us -> 0 us
  other arithmetic: 53.7 us -> 0 us
  starting transfers between devices: 49.2 us -> 0 us
  local copies, waits for them, and re-layouts: 50.6 us -> 3.69 us
  between operations: 14.9 us -> 0.01 us
    ppermute x17 -> x0, waiting for transfers between devices: 435 us -> none  [passed_along(): return lax.ppermute(block, axis, route)]
    pallas_call x0 -> x1, Pallas kernels: none -> 143 us  [shards(): pl.pallas_call(functools.partial(kernel, var_count, segments, rows_of_x),...]
    dot_general x46 -> x0, matrix products: 79.6 us -> none  [the longest x9 32 us: block_terms(): jnp.einsum('phe,qhe->hpq', own_grad, value_block, preferred_element_type=...]
    ppermute x17 -> x0, starting transfers between devices: 49.2 us -> none  [passed_along(): return lax.ppermute(block, axis, route)]
    slice x24 -> x0, local copies, waits for them, and re-layouts: 41 us -> none  [the longest x16 32.6 us: shards(): pair_block[1].reshape(token_shape)]
    convert_element_type x3 -> x0, other arithmetic: 38.5 us -> none  [the longest x2 35 us: shards(): (score_scale * attention * (grad_attn - row_delta[:, :, None])).astype(jn...]
    another operation x9 -> x0, other arithmetic: 7.05 us -> none  [the longest x8 4.7 us: shards(): jnp.stack([key_part.reshape(patches, feature_width), value_part.reshape(p...]
  transfers between devices with their start and end apart: 18 -> 0, of which waited for: 10 -> 0; matrix products, arithmetic and copies ran while one was open for 25% -> 0% of each run, Pallas kernels for 0% -> 0%
where the time goes in v1:
time: 149 us; the launch traced here: 147 us
  Pallas kernels  143 us (96%)
  local copies, waits for them, and re-layouts  3.69 us (2%)
    pallas_call x1, Pallas kernels, shards(): pl.pallas_call(functools.partial(kernel, var_count, segments, rows_of_x),...  143 us
    unnamed x4, local copies, waits for them, and re-layouts  3.69 us

profile of v1, /device:TPU:88, one launch (start us, length us, event | category | flops | bytes accessed | tf_op | source)
XLA Modules:
  0.0 146.9 jit_solution(8761826321992620939)
XLA Ops:
  0.0 0.0 copy-start
  0.0 0.7 copy-done
  0.7 0.7 copy.7.links
  1.4 143.2 %shard_map.64 = bf16[256,2048]{1,0:T(8,128)(2,1)} custom-call(s32[32,9]{1,0:T(8,128)} %copy.7.links, bf16[256,1024]{1,0:T(8,128)(2,1)} %bitcast.7, bf16[256,1024]{1,0:T(8,128)(2,1)} %bitcast.8, bf16[256,1024]{1,0:T(8,128)(2,1)} %bitcast.9, bf16[256,1024]{1,0:T(8,128)(2,1)} %bitcast.10, bf16[2,32,3072]{2,1,0:T(8,128)(2,1)} %bitcast.11), custom_call_target="tpu_custom_call" | custom-call | tf_op jit(solution)/shard_map/pallas_call | solution.py:484
  144.6 2.3 %copy.9 = bf16[1,1,1,256,2048]{4,3,2,1,0:T(8,128)(2,1)} copy(bf16[1,1,1,256,2048]{4,3,2,1,0:T(8,128)(2,1)} %bitcast.6) | data formatting | bytes 2097152
Async XLA Ops:
  0.0 0.7 copy-start

commit v2 on v1

--- a/solution.py
+++ b/solution.py
@@ -109,7 +109,7 @@
 
 
 def linked_row(links, gv, var_count):
-    entries = [links[gv, j] for j in range(WINDOW)]
+    entries = [links[j, gv] for j in range(WINDOW)]
     linked = []
     for w in range(WINDOW):
         target = mod(gv + w - REACH, var_count)
@@ -127,7 +127,7 @@
 
 def kernel(var_count, segments, rows_of_x, links, q_in, k_in, v_in, o_in, w_in, out,
            kbuf, vbuf, kT, qbuf, obuf, qc, oc, p_s, a_s, st, dkacc, dvacc, dqout,
-           kvout, back, grads, wbuf,
+           kvout, back, grads, wbuf, sums, row_sem,
            in_send, in_recv, own_sem, halo_send, halo_recv, dq_send, dq_recv,
            back_send, back_recv, kv_send, kv_recv,
            wy_send, wy_recv, wz_send, wz_recv, wx_send, wx_recv, wf_send, wf_recv, wc_send, wc_recv):
@@ -153,17 +153,28 @@
         greet(at(x, z + d))
         return 0
 
-    def greet_y(d, _):
-        greet({"var": x * ROW + mod(z + d, ROW), "segment": seg_down})
-        greet({"var": x * ROW + mod(z + d, ROW), "segment": seg_up})
-        return 0
-
     lax.fori_loop(1, ROW, greet_z, 0)
     greet(at(x + 1, z))
     greet(at(x - 1, z))
     greet({"dp": 1 - core})
-    lax.fori_loop(0, ROW, greet_y, 0)
-    pl.semaphore_wait(barrier, (ROW - 1) + 3 + 2 * ROW)
+    greet({"segment": seg_down})
+    greet({"segment": seg_up})
+
+    def columns(zz):
+        return pl.ds(pl.multiple_of(zz * LANES, LANES), LANES)
+
+    ins = ((k_in, kbuf, REACH), (v_in, vbuf, REACH), (q_in, qbuf, 0), (o_in, obuf, 0))
+
+    def own(kind):
+        src, dst, first = ins[kind]
+        return pltpu.make_async_copy(src.at[:, columns(z)], dst.at[first + z], own_sem.at[kind])
+
+    for kind in range(4):
+        own(kind).start()
+    dkacc[...] = jnp.zeros_like(dkacc)
+    dvacc[...] = jnp.zeros_like(dvacc)
+    pl.semaphore_wait(barrier, (ROW - 1) + 5)
+    pl.semaphore_signal(row_sem, inc=1, device_id={"segment": seg_up}, device_id_type=MESH)
 
     def remote(src, dst, send, recv, where):
         return pltpu.make_async_remote_copy(
@@ -234,15 +245,6 @@
 
     w_down().start()
 
-    def columns(zz):
-        return pl.ds(pl.multiple_of(zz * LANES, LANES), LANES)
-
-    ins = ((k_in, kbuf, REACH), (v_in, vbuf, REACH), (q_in, qbuf, 0), (o_in, obuf, 0))
-
-    def own(kind):
-        src, dst, first = ins[kind]
-        return pltpu.make_async_copy(src.at[:, columns(z)], dst.at[first + z], own_sem.at[kind])
-
     def to_peer(kind, d):
         src, dst, first = ins[kind]
         return remote(src.at[:, columns(mod(z + d, ROW))], dst.at[first + z],
@@ -253,9 +255,6 @@
         return remote(src.at[:, columns(z)], dst.at[first + mod(z - d, ROW)],
                       in_send.at[kind, d], in_recv.at[kind, d], at(x, z + d))
 
-    for kind in range(4):
-        own(kind).start()
-
     def send_kv(j, _):
         d = ring_order(j)
         to_peer(0, d).start()
@@ -268,9 +267,10 @@
         to_peer(3, d).start()
         return 0
 
+    w_own()
+    w_z_arrived(1)
+    w_z_arrived(7)
     lax.fori_loop(0, ROW - 1, send_kv, 0)
-    lax.fori_loop(0, ROW - 1, send_qo, 0)
-    w_own()
 
     def halo(kind, zs):
         buf = (kbuf, vbuf)[kind]
@@ -282,18 +282,30 @@
         own(kind).wait()
         halo(kind, z).start()
 
-    dkacc[...] = jnp.zeros_like(dkacc)
-    dvacc[...] = jnp.zeros_like(dvacc)
-
     def take_kv(j, _):
-        d = ring_order(6 - j)
+        d = ring_order(j)
         zs = mod(z - d, ROW)
         for kind in range(2):
             from_peer(kind, d).wait_recv()
             halo(kind, zs).start()
         return 0
 
-    lax.fori_loop(0, ROW - 1, take_kv, 0)
+    w_x_arrived(0)
+    w_z_arrived(2)
+    w_z_arrived(6)
+    w_f_arrived(0)
+    w_x_arrived(1)
+    w_x_arrived(7)
+    lax.fori_loop(0, 3, take_kv, 0)
+    lax.fori_loop(0, 3, send_qo, 0)
+    w_z_arrived(3)
+    w_z_arrived(5)
+    lax.fori_loop(3, ROW - 1, send_qo, 0)
+    lax.fori_loop(3, ROW - 1, take_kv, 0)
+    w_x_arrived(2)
+    w_x_arrived(6)
+    w_f_arrived(1)
+    w_f_arrived(7)
 
     def turn(slot):
         kT[slot] = kbuf[slot].T
@@ -316,6 +328,7 @@
     lax.fori_loop(0, ROW, take_halo, 0)
     own(2).wait()
     own(3).wait()
+    pl.semaphore_wait(row_sem, 1)
 
     refs = (kbuf, vbuf, kT, qbuf, obuf, qc, oc, p_s, a_s, st, dkacc, dvacc, dqout)
 
@@ -338,50 +351,44 @@
         def _():
             dq_home(ring_order(8 - j)).start()
 
-        for when, work in {2: (1, 7), 3: (2, 6), 4: (3, 5), 5: (4,)}.items():
+        plan = {
+            0: [(w_z_arrived, 4)],
+            2: [(w_x_arrived, 3), (w_x_arrived, 5)],
+            4: [(w_f_arrived, 2), (w_f_arrived, 6), (w_x_arrived, 4)],
+            6: [(w_f_arrived, 3), (w_f_arrived, 5)],
+        }
+        for when, work in plan.items():
             @pl.when(j == when)
             def _(work=work):
-                for r in work:
-                    w_z_arrived(r)
-
-        for when, work in {3: (0,), 5: (1,), 6: (7,), 7: (2,)}.items():
-            @pl.when(j == when)
-            def _(work=work):
-                for r in work:
-                    w_x_arrived(r)
+                for act, *args in work:
+                    act(*args)
 
         second_pass(v, linked_row(links, x * ROW + v, var_count), refs)
         return 0
 
     lax.fori_loop(0, ROW, step, 0)
 
-    def out_halo(j):
-        return j + ROW * (j // REACH)
+    def send_back(kind, zs):
+        slot = lax.rem(zs + 12, SLOTS)
+        return remote(kvout.at[kind, slot], back.at[kind, zs], back_send.at[kind, zs], back_recv.at[kind, zs],
+                      at(x + 1 - 2 * (zs // REACH), z))
 
     def cast_halo(j, _):
-        slot = out_halo(j)
+        slot = lax.rem(mod(z - ring_order(j), ROW) + 12, SLOTS)
         kvout[0, slot] = dkacc[slot].astype(BF16)
         kvout[1, slot] = dvacc[slot].astype(BF16)
-        return 0
-
-    def send_back(kind, j):
-        slot = out_halo(j)
-        zs = lax.rem(slot + 4, SLOTS)
-        up = j // REACH
-        return remote(kvout.at[kind, slot], back.at[kind, zs], back_send.at[kind, zs], back_recv.at[kind, zs],
-                      at(x + 2 * up - 1, z))
+
+        @pl.when(j > 0)
+        def _():
+            for kind in range(2):
+                send_back(kind, mod(z - ring_order(j - 1), ROW)).start()
+
+        return 0
 
     lax.fori_loop(0, ROW, cast_halo, 0)
-
-    def start_back(j, _):
-        send_back(0, j).start()
-        send_back(1, j).start()
-        return 0
-
-    lax.fori_loop(0, ROW, start_back, 0)
     dq_home(REACH).start()
-    w_x_arrived(6)
-    w_f_arrived(0)
+    send_back(0, z).start()
+    send_back(1, z).start()
 
     def from_back(kind, zs):
         return remote(kvout.at[kind, 0], back.at[kind, zs], back_send.at[kind, zs], back_recv.at[kind, zs],
@@ -411,38 +418,67 @@
         return 0
 
     lax.fori_loop(0, ROW, send_home, 0)
-    for r in (3, 5, 4):
-        w_x_arrived(r)
-        if r == 3:
-            kv_home(0, 0).start()
-            kv_home(1, 0).start()
-    for r in ARRIVAL[1:]:
-        w_f_arrived(r)
+    kv_home(0, 0).start()
+    kv_home(1, 0).start()
+    w_f_arrived(4)
 
     for r in range(ROW):
         for xs in range(4):
             w_c_arrives(xs, r).wait_recv()
 
-    def grads_arrive(d, _):
-        zs = mod(z + d, ROW)
-        remote(dqout.at[0], grads.at[:, columns(zs)], dq_send.at[d], dq_recv.at[d], at_down(z)).wait_recv()
+    def dq_arrives(d, _):
+        remote(dqout.at[0], grads.at[:, columns(mod(z + d, ROW))], dq_send.at[d], dq_recv.at[d], at_down(z)).wait_recv()
+        return 0
+
+    def kv_columns(kind, zs):
+        return pl.ds(pl.multiple_of((kind + 1) * ROW * LANES + zs * LANES, LANES), LANES)
+
+    def kv_arrives(j, _):
+        d = ring_order(j)
         for kind in range(2):
-            col = pl.ds(pl.multiple_of((kind + 1) * ROW * LANES + zs * LANES, LANES), LANES)
-            remote(kvout.at[kind, 0], grads.at[:, col], kv_send.at[kind, d], kv_recv.at[kind, d],
-                   at_down(z)).wait_recv()
-        return 0
-
-    lax.fori_loop(0, ROW, grads_arrive, 0)
+            remote(kvout.at[kind, 0], grads.at[:, kv_columns(kind, mod(z + d, ROW))],
+                   kv_send.at[kind, d], kv_recv.at[kind, d], at_down(z)).wait_recv()
+        return 0
 
     chunk = 4
-
-    def project(c, _):
-        w = wbuf[pl.ds(c * chunk, chunk)].reshape(chunk * 64, wbuf.shape[3])
-        cols = pl.ds(pl.multiple_of(c * chunk * 64, chunk * 64), chunk * 64)
-        out[:, cols] = dot(grads[...], w, 1, 1).astype(BF16)
-        return 0
-
-    lax.fori_loop(0, wbuf.shape[0] // chunk, project, 0)
+    width = chunk * 64
+
+    def out_columns(c):
+        return pl.ds(pl.multiple_of(c * width, width), width)
+
+    lax.fori_loop(0, ROW, dq_arrives, 0)
+
+    def project_q(c, _):
+        w = wbuf[pl.ds(c * chunk, chunk), :, :, 0 : ROW * LANES].reshape(width, ROW * LANES)
+        sums[:, out_columns(c)] = dot(grads[:, 0 : ROW * LANES], w, 1, 1)
+        return 0
+
+    lax.fori_loop(0, wbuf.shape[0] // chunk, project_q, 0)
+
+    def project_kv(first, c):
+        part = sums[:, out_columns(c)]
+        for j in range(first, first + 4):
+            zs = mod(z + ring_order(j), ROW)
+            cols = [kv_columns(kind, zs) for kind in range(2)]
+            w = [wbuf[pl.ds(c * chunk, chunk), :, :, col].reshape(width, LANES) for col in cols]
+            g = [grads[:, col] for col in cols]
+            part += dot(jnp.concatenate(g, axis=1), jnp.concatenate(w, axis=1), 1, 1)
+        return part
+
+    lax.fori_loop(0, 4, kv_arrives, 0)
+
+    def project_far(c, _):
+        sums[:, out_columns(c)] = project_kv(0, c)
+        return 0
+
+    lax.fori_loop(0, wbuf.shape[0] // chunk, project_far, 0)
+    lax.fori_loop(4, ROW, kv_arrives, 0)
+
+    def project_near(c, _):
+        out[:, out_columns(c)] = project_kv(4, c).astype(BF16)
+        return 0
+
+    lax.fori_loop(0, wbuf.shape[0] // chunk, project_near, 0)
 
     def left_z(d, _):
         for kind in range(4):
@@ -504,6 +540,8 @@
             pltpu.VMEM((2, ROW) + block, BF16),
             pltpu.VMEM((patches, cols), BF16),
             pltpu.VMEM((var_count, 2, rows // 2, cols), BF16),
+            pltpu.VMEM((patches, var_count * rows), F32),
+            pltpu.SemaphoreType.REGULAR,
             dma((4, ROW)), dma((4, ROW)), dma((4,)), dma((2, ROW)), dma((2, ROW)), dma((ROW,)), dma((ROW,)),
             dma((2, ROW)), dma((2, ROW)), dma((2, ROW)), dma((2, ROW)),
             dma(()), dma(()), dma((ROW,)), dma((ROW,)), dma((2, ROW)), dma((2, ROW)),
@@ -513,7 +551,7 @@
             collective_id=0, has_side_effects=True, vmem_limit_bytes=60 * 1024 * 1024
         ),
     )(
-        links,
+        links.T,
         queries.reshape(patches, width),
         keys.reshape(patches, width),
         values.reshape(patches, width),

time: 149 us -> 134 us (0.90)
  Pallas kernels: 143 us -> 131 us
    pallas_call x1, Pallas kernels: 143 us -> 131 us  [shards(): pl.pallas_call(functools.partial(kernel, var_count, segments, rows_of_x),...]
    unnamed x4 -> x1, local copies, waits for them, and re-layouts: 3.69 us -> 2.3 us
where the time goes in v2:
time: 134 us; the launch traced here: 133 us
  Pallas kernels  131 us (98%)
  local copies, waits for them, and re-layouts  2.3 us (2%)
    pallas_call x1, Pallas kernels, shards(): pl.pallas_call(functools.partial(kernel, var_count, segments, rows_of_x),...  131 us

profile of v2, /device:TPU:88, one launch (start us, length us, event | category | flops | bytes accessed | tf_op | source)
XLA Modules:
  0.0 132.8 jit_solution(14387491701082422771)
XLA Ops:
  0.0 130.5 %shard_map.64 = bf16[256,2048]{1,0:T(8,128)(2,1)} custom-call(s32[9,32]{1,0:T(8,128)} %bitcast.13, bf16[256,1024]{1,0:T(8,128)(2,1)} %bitcast.8, bf16[256,1024]{1,0:T(8,128)(2,1)} %bitcast.9, bf16[256,1024]{1,0:T(8,128)(2,1)} %bitcast.10, bf16[256,1024]{1,0:T(8,128)(2,1)} %bitcast.11, bf16[2,32,3072]{2,1,0:T(8,128)(2,1)} %bitcast.12), custom_call_target="tpu_custom_call" | custom-call | tf_op jit(solution)/shard_map/pallas_call | solution.py:520
  130.5 2.3 %copy.8 = bf16[1,1,1,256,2048]{4,3,2,1,0:T(8,128)(2,1)} copy(bf16[1,1,1,256,2048]{4,3,2,1,0:T(8,128)(2,1)} %bitcast.7) | data formatting | bytes 2097152
